TPU v7x, 256 devices: a whole 4x4x8 slice. The times are simulated.
256 devices in a mesh: rep: 2 (over z_hi), dp: 32 (over z_lo, x, core), mp: 4 (over y).
Axes of the slice: x: 4, y: 4, z: 8 (z_hi: 2, z_lo: 4; z = z_hi * 4 + z_lo), core: 2. Of those that a mesh axis runs over, the one named last changes fastest.
Arguments:
- tokens: bfloat16 [24576, 2048], P(('rep', 'dp', 'mp')), may hold values from -6 to 6
- request_ids: int32 [64, 384], P(('rep', 'dp')), may hold values from 0 to 7, never falling along the last dimension, each value on 1 to 192 neighbouring positions
- cache_entries: bfloat16 [32768, 4096], P(('rep', 'dp', 'mp')), may hold values from -250 to 250, as said below
- cached_lengths: int32 [64, 8], replicated, may hold values from 1 to 256, 512 in all within a row
- traded: int32 [32], P('dp'), may hold values from 0 to 1, as said below
- query_weight: bfloat16 [2048, 2048], P(None, 'mp'), may hold values from -0.125 to 0.125
- key_weight: bfloat16 [2048, 2048], P(None, 'mp'), may hold values from -0.125 to 0.125
- value_weight: bfloat16 [2048, 2048], P(None, 'mp'), may hold values from -0.125 to 0.125
- output_weight: bfloat16 [2048, 2048], P('mp'), may hold values from -0.125 to 0.125
- gate_weight: bfloat16 [2048, 8192], P('dp', 'mp'), may hold values from -0.125 to 0.125
- up_weight: bfloat16 [2048, 8192], P('dp', 'mp'), may hold values from -0.125 to 0.125
- down_weight: bfloat16 [2048, 8192], P('dp', 'mp'), may hold values from -0.0625 to 0.0625
Outputs:
- layer_output: bfloat16 [24576, 2048], P(('rep', 'dp', 'mp'))
Inputs may be any that keep to these rules, and one draw needn't show every extreme that they name: `request_ids`: each group's row never falls; every request 0 to 7 has 1 to 192 new tokens in each group, some request exactly 192. `cached_lengths`: each row sums to 512; its largest entry is 256. `traded`: exactly 16 entries are 1. `cache_entries`: keys are stored already rotated to their positions; rows of cache group g are g * 512 to (g + 1) * 512 - 1, the requests' prefixes in request order.
All inputs are finite; a program needn't handle non-finite values.
Results may differ from a plain program's by a relative error of at most 0.013.
The roundings to bfloat16 on the way count: a program that leaves them out, or rounds other values in their place, can miss the bound.
Values may be sent and summed in bfloat16 or wider, within the bound.
A program may use at most 128 MiB of HBM per device.

v0:
```python
import math
import jax
import jax.numpy as jnp
from jax import lax
from jax.sharding import PartitionSpec as P

D = 2048
HEADS = 16
HEAD_DIM = 128
TOK_GROUP = 384
CACHE = 512
EPSILON = 1e-05
ROPE_BASE = 10000.0


def swapped(value, axis, apart):
    mask = 2**apart
    pairs = [(source, source ^ mask) for source in range(lax.axis_size(axis))]
    return lax.ppermute(value, axis, pairs)


def layer_norm(rows):
    center = rows - jnp.mean(rows, axis=-1, keepdims=True)
    spread = jnp.mean(center * center, axis=-1, keepdims=True)
    return center * lax.rsqrt(spread + EPSILON)


def request_layout(request_row, length_row, cache_size):
    number = length_row.shape[0]
    labels = jnp.arange(number, dtype=jnp.int32)
    onehot = (request_row[:, None] == labels[None, :]).astype(jnp.int32)
    counts = jnp.sum(onehot, axis=0)
    starts = jnp.cumsum(counts) - counts
    token_place = jnp.arange(request_row.shape[0], dtype=jnp.int32)
    positions = jnp.sum(onehot * (length_row - starts)[None, :], axis=1) + token_place
    bounds = jnp.cumsum(length_row)
    cache_place = jnp.arange(cache_size, dtype=jnp.int32)
    owner = jnp.sum((cache_place[:, None] >= bounds[None, :]).astype(jnp.int32), axis=1)
    return (positions, owner)


def rotate(vectors, positions):
    half = vectors.shape[-1] // 2
    freq = ROPE_BASE ** (-jnp.arange(half, dtype=jnp.float32) / half)
    angle = positions.astype(jnp.float32)[:, None] * freq[None, :]
    cosine = jnp.cos(angle)[:, None, :]
    sine = jnp.sin(angle)[:, None, :]
    first = vectors[..., :half]
    second = vectors[..., half:]
    return jnp.concatenate(
        [first * cosine - second * sine, second * cosine + first * sine], axis=-1
    )


def attend(query, keys_new, values_new, keys_cache, values_cache, request_row, owner):
    scale = 1.0 / math.sqrt(query.shape[-1])
    keys = jnp.concatenate([keys_cache, keys_new], axis=0)
    values = jnp.concatenate([values_cache, values_new], axis=0)
    scores = jnp.einsum("thd,khd->htk", query, keys, preferred_element_type=jnp.float32) * scale
    count = request_row.shape[0]
    place = jnp.arange(count, dtype=jnp.int32)
    same_cache = owner[None, :] == request_row[:, None]
    same_new = (request_row[None, :] == request_row[:, None]) & (place[None, :] <= place[:, None])
    allowed = jnp.concatenate([same_cache, same_new], axis=1)
    scores = jnp.where(allowed[None], scores, -1e30)
    top = jnp.max(scores, axis=-1, keepdims=True)
    raised = jnp.exp(scores - top)
    total = jnp.sum(raised, axis=-1, keepdims=True)
    weights = (raised / total).astype(jnp.bfloat16)
    mixed = jnp.einsum("htk,khd->thd", weights, values, preferred_element_type=jnp.float32)
    return mixed.astype(jnp.bfloat16)


def local(
    tokens,
    request_ids,
    cache_entries,
    cached_lengths,
    traded,
    query_weight,
    key_weight,
    value_weight,
    output_weight,
    gate_weight,
    up_weight,
    down_weight,
):
    tensor_size = lax.axis_size("mp")
    local_heads = HEADS // tensor_size
    replica = lax.axis_index("rep")
    within = lax.axis_index("dp")
    pairs = lax.axis_size("dp")
    group = replica * pairs + within
    moved_here = traded[0] == 1
    source = jnp.where(moved_here, (1 - replica) * pairs + within, group)
    length_row = lax.dynamic_slice_in_dim(cached_lengths, source, 1, 0)[0]
    request_row = request_ids[0]
    partner = swapped(cache_entries, "rep", 0)
    stored = jnp.where(moved_here, partner, cache_entries)
    by_heads = lax.all_to_all(
        stored.reshape(stored.shape[0], 2, D), "mp", split_axis=2, concat_axis=0, tiled=True
    )
    keys_cache = by_heads[:, 0].reshape(CACHE, local_heads, HEAD_DIM)
    values_cache = by_heads[:, 1].reshape(CACHE, local_heads, HEAD_DIM)
    rows_full = lax.all_gather(tokens, "mp", axis=0, tiled=True)
    positions, owner = request_layout(request_row, length_row, CACHE)
    normed = layer_norm(rows_full.astype(jnp.float32)).astype(jnp.bfloat16)
    query = jnp.dot(normed, query_weight, preferred_element_type=jnp.float32).reshape(
        TOK_GROUP, local_heads, HEAD_DIM
    )
    query = rotate(query, positions).astype(jnp.bfloat16)
    keys_new = jnp.dot(normed, key_weight, preferred_element_type=jnp.float32).reshape(
        TOK_GROUP, local_heads, HEAD_DIM
    )
    keys_new = rotate(keys_new, positions).astype(jnp.bfloat16)
    values_new = (
        jnp.dot(normed, value_weight, preferred_element_type=jnp.float32)
        .astype(jnp.bfloat16)
        .reshape(TOK_GROUP, local_heads, HEAD_DIM)
    )
    mixed = attend(query, keys_new, values_new, keys_cache, values_cache, request_row, owner)
    mixed = mixed.reshape(TOK_GROUP, local_heads * HEAD_DIM)
    own_sum = lax.psum_scatter(
        jnp.dot(mixed, output_weight, preferred_element_type=jnp.float32),
        "mp",
        scatter_dimension=0,
        tiled=True,
    )
    state_own = (tokens.astype(jnp.float32) + own_sum).astype(jnp.bfloat16)
    normed_own = layer_norm(state_own.astype(jnp.float32)).astype(jnp.bfloat16)
    normed_two = lax.all_gather(normed_own, "mp", axis=0, tiled=True)

    def add_rows(piece):
        return jnp.dot(normed_two, piece, preferred_element_type=jnp.float32)

    gate = add_rows(lax.all_gather(gate_weight, "dp", axis=0, tiled=True))
    upward = add_rows(lax.all_gather(up_weight, "dp", axis=0, tiled=True))
    activated = (jax.nn.silu(gate) * upward).astype(jnp.bfloat16)
    terms = lax.dot_general(
        activated,
        lax.all_gather(down_weight, "dp", axis=0, tiled=True),
        (((1,), (1,)), ((), ())),
        preferred_element_type=jnp.float32,
    )
    hidden_own = lax.psum_scatter(terms, "mp", scatter_dimension=0, tiled=True)
    return (state_own.astype(jnp.float32) + hidden_own).astype(jnp.bfloat16)


def solution(mesh):
    in_specs = (
        P(("rep", "dp", "mp"), None),
        P(("rep", "dp"), None),
        P(("rep", "dp", "mp"), None),
        P(),
        P("dp"),
        P(None, "mp"),
        P(None, "mp"),
        P(None, "mp"),
        P("mp", None),
        P("dp", "mp"),
        P("dp", "mp"),
        P("dp", "mp"),
    )
    out_specs = P(("rep", "dp", "mp"), None)
    return jax.shard_map(local, mesh=mesh, in_specs=in_specs, out_specs=out_specs, check_vma=False)
```

profile of v0, /device:TPU:1, one launch (start us, length us, event | category | flops | bytes accessed | tf_op | source)
XLA Modules:
  0.0 476.3 jit_solution(9177185737929228484)
XLA Ops:
  6.5 1.8 copy.71
  8.3 7.8 %collective-permute-start = (bf16[128,4096]{0,1:T(8,128)(2,1)S(1)}, bf16[128,4096]{0,1:T(8,128)(2,1)}, u32[]{:S(2)}, u32[]{:S(2)}) collective-permute-start(bf16[128,4096]{0,1:T(8,128)(2,1)S(1)} %copy.71), channel_id=1, source_target_pairs={{0,128},{128,0},{1,129},{129,1},{2,130},{130,2},{3,131},{131,3},{4... | collective-permute-start | bytes 3145736 | tf_op jit(solution)/shard_map/ppermute | solution.py:19
  16.1 0.0 all-gather.6.cloned.1.call-update
  16.8 0.8 constant_dynamic-slice_fusion
  17.6 0.1 copy.86
  17.7 0.7 reduce
  18.4 0.1 convert_reduce_fusion.3
  18.5 0.2 reduce-window_1_clone.1
  18.7 0.2 reduce-window.9
  18.8 0.1 convert_reduce_fusion.2
  18.9 0.1 select_reduce_fusion
  19.0 0.2 broadcast_compare_fusion
  19.2 25.3 %collective-permute-done = bf16[128,4096]{0,1:T(8,128)(2,1)} collective-permute-done((bf16[128,4096]{0,1:T(8,128)(2,1)S(1)}, bf16[128,4096]{0,1:T(8,128)(2,1)}, u32[]{:S(2)}, u32[]{:S(2)}) %collective-permute-start) | collective-permute-done | bytes 1048608 | tf_op jit(solution)/shard_map/ppermute | solution.py:19
  44.6 1.3 broadcast_select_fusion
  45.9 9.5 %copy.73 = bf16[128,2,2048]{0,1,2:T(2,128)(2,1)} copy(bf16[128,2,2048]{0,2,1:T(8,128)(2,1)S(1)} %bitcast.28) | data formatting | bytes 2097152 | tf_op jit(solution)/shard_map/reshape | solution.py:101
  55.4 4.7 all-to-all-start
  60.1 0.1 fusion.26
  60.2 0.8 pad_add_fusion
  61.0 1.5 multiply_cosine_fusion
  62.5 7.3 %all-to-all-done = bf16[128,2,2048]{0,1,2:T(2,128)(2,1)S(1)} async-done(((bf16[128,2,2048]{0,1,2:T(2,128)(2,1)}), bf16[128,2,2048]{0,1,2:T(2,128)(2,1)S(1)}, u32[]{:S(2)}, u32[]{:S(2)}) %all-to-all-start) | async-done | bytes 1048608 | tf_op jit(solution)/shard_map/all_to_all | solution.py:100
  69.8 1.1 copy.74
  70.9 1.5 copy.75
  72.4 1.0 fusion.40
  73.5 1.3 copy.81
  74.7 0.3 copy.84
  75.0 2.0 copy.76
  77.0 1.8 convert_reduce_fusion
  78.9 2.0 fusion.4
  80.8 3.6 fusion.35
  84.4 1.4 reshape.153
  85.8 4.0 fusion.37
  89.8 2.3 reshape.151
  92.1 3.9 convolution_convert_fusion
  95.9 1.9 copy.85
  97.8 2.3 fusion.41
  100.2 0.4 subtract_convert_fusion.1
  100.6 0.9 fusion.16
  101.5 0.0 copy-done.8
  101.6 2.7 fusion.43
  104.3 1.1 fusion.10
  105.4 2.7 fusion.44
  108.1 0.0 reduce-scatter.3.cloned.1.call-update
  108.1 0.3 all-gather.8.cloned.1.call-start
  108.4 61.6 %reduce-scatter.3.cloned.1.call-done = f32[96,2048]{1,0:T(8,128)} async-done(((f32[384,2048]{1,0:T(8,128)}), f32[96,2048]{1,0:T(8,128)}) %reduce-scatter.3.cloned.1.call-update) | async-done | bytes 786448 | tf_op jit(solution)/shard_map/reduce_scatter | solution.py:123
  169.9 1.3 convert_reduce_fusion.1
  171.3 0.3 fusion.22
  171.6 1.0 fusion.23
  172.5 0.0 all-gather.8.cloned.1.call-update
  172.6 0.0 all-gather.10.cloned.1.call-start
  172.6 0.5 all-gather.10.cloned.1.call-update
  173.1 0.0 all-gather.12.cloned.1.call-start
  173.2 0.5 all-gather.12.cloned.1.call-update
  173.7 0.0 all-gather.14.cloned.1.call-start
  173.8 0.5 all-gather.14.cloned.1.call-update
  174.3 0.0 reduce-scatter.5.cloned.1.call-start
  174.4 27.1 %all-gather.8.cloned.1.call-done = bf16[384,2048]{1,0:T(8,128)(2,1)} async-done(((bf16[96,2048]{1,0:T(8,128)(2,1)}), bf16[384,2048]{1,0:T(8,128)(2,1)}) %all-gather.8.cloned.1.call-update) | async-done | bytes 1572880 | tf_op jit(solution)/shard_map/all_gather | solution.py:131
  201.5 71.4 %all-gather.10.cloned.1.call-done = bf16[2048,2048]{1,0:T(8,128)(2,1)} async-done(((bf16[64,2048]{1,0:T(8,128)(2,1)}), bf16[2048,2048]{1,0:T(8,128)(2,1)}) %all-gather.10.cloned.1.call-update) | async-done | bytes 8388624 | tf_op jit(solution)/shard_map/all_gather | solution.py:136
  272.9 9.0 %fusion.45 = f32[384,2048]{1,0:T(8,128)} fusion(bf16[384,2048]{1,0:T(8,128)(2,1)} %all-gather.8.cloned.1.call-done, bf16[2048,2048]{1,0:T(8,128)(2,1)} %all-gather.10.cloned.1.call-done), kind=kOutput, calls=%fused_computation.76 | convolution fusion | flops 3221225472 | bytes 13107200 | tf_op jit(solution)/shard_map/dot_general | solution.py:134
  281.9 60.6 %all-gather.12.cloned.1.call-done = bf16[2048,2048]{1,0:T(8,128)(2,1)} async-done(((bf16[64,2048]{1,0:T(8,128)(2,1)}), bf16[2048,2048]{1,0:T(8,128)(2,1)}) %all-gather.12.cloned.1.call-update) | async-done | bytes 8388624 | tf_op jit(solution)/shard_map/all_gather | solution.py:137
  342.5 69.7 %all-gather.14.cloned.1.call-done = bf16[2048,2048]{1,0:T(8,128)(2,1)} async-done(((bf16[64,2048]{1,0:T(8,128)(2,1)}), bf16[2048,2048]{1,0:T(8,128)(2,1)}) %all-gather.14.cloned.1.call-update) | async-done | bytes 8388624 | tf_op jit(solution)/shard_map/all_gather | solution.py:141
  412.2 15.9 %fusion.25 = f32[384,2048]{1,0:T(8,128)} fusion(bf16[2048,2048]{1,0:T(8,128)(2,1)} %all-gather.14.cloned.1.call-done, f32[384,2048]{1,0:T(8,128)} %fusion.45, bf16[384,2048]{1,0:T(8,128)(2,1)} %all-gather.8.cloned.1.call-done, bf16[2048,2048]{1,0:T(8,128)(2,1)} %all-gather.12.cloned.1.call-done), kind=kOutput, calls=%fused_computation.42 | convolution fusion | flops 6447169536 | bytes 24641536 | tf_op jit(solution)/shard_map/dot_general | solution.py:139
  428.1 0.0 reduce-scatter.5.cloned.1.call-update
  428.1 39.4 %reduce-scatter.5.cloned.1.call-done = f32[96,2048]{1,0:T(8,128)} async-done(((f32[384,2048]{1,0:T(8,128)}), f32[96,2048]{1,0:T(8,128)}) %reduce-scatter.5.cloned.1.call-update) | async-done | bytes 786448 | tf_op jit(solution)/shard_map/reduce_scatter | solution.py:145
  467.5 2.0 fusion.24
  (27 shorter events, 0.1 us)
Async XLA Ops:
  6.5 98.8 %copy-start = (bf16[512,2048]{1,0:T(8,128)(2,1)S(1)}, bf16[512,2048]{1,0:T(8,128)(2,1)}, u32[]{:S(2)}) copy-start(bf16[512,2048]{1,0:T(8,128)(2,1)} %param.20) | copy-start | bytes 6291460
  6.5 70.5 %all-gather.6.cloned.1.call-start = ((), (), s32[]{:S(2)}) async-start(), calls=%async_computation.3 | async-start | bytes 1966080 | tf_op jit(solution)/shard_map/all_gather | solution.py:105
  8.3 36.3 %collective-permute-start = (bf16[128,4096]{0,1:T(8,128)(2,1)S(1)}, bf16[128,4096]{0,1:T(8,128)(2,1)}, u32[]{:S(2)}, u32[]{:S(2)}) collective-permute-start(bf16[128,4096]{0,1:T(8,128)(2,1)S(1)} %copy.71), channel_id=1, source_target_pairs={{0,128},{128,0},{1,129},{129,1},{2,130},{130,2},{3,131},{131,3},{4... | collective-permute-start | bytes 3145736 | tf_op jit(solution)/shard_map/ppermute | solution.py:19
  55.4 14.5 %all-to-all-start = ((bf16[128,2,2048]{0,1,2:T(2,128)(2,1)}), bf16[128,2,2048]{0,1,2:T(2,128)(2,1)S(1)}, u32[]{:S(2)}, u32[]{:S(2)}) async-start(bf16[128,2,2048]{0,1,2:T(2,128)(2,1)} %copy.73), calls=%async_computation | async-start | bytes 2097152 | tf_op jit(solution)/shard_map/all_to_all | solution.py:100
  60.1 109.8 %reduce-scatter.3.cloned.1.call-start = ((), (), s32[]{:S(2)}) async-start(), calls=%async_computation.4 | async-start | bytes 3932160 | tf_op jit(solution)/shard_map/reduce_scatter | solution.py:123
  77.0 3.8 copy-start.2
  97.8 2.3 copy-start.4
  97.8 2.3 copy-start.5
  100.6 1.0 copy-start.8
  101.6 2.7 copy-start.6
  101.6 2.7 copy-start.7
  105.4 64.5 %copy-start.3 = (bf16[96,2048]{1,0:T(8,128)(2,1)S(1)}, bf16[96,2048]{1,0:T(8,128)(2,1)}, u32[]{:S(2)}) copy-start(bf16[96,2048]{1,0:T(8,128)(2,1)} %param.12) | copy-start | bytes 1179652
  108.1 93.4 %all-gather.8.cloned.1.call-start = ((), (), s32[]{:S(2)}) async-start(), calls=%async_computation.5 | async-start | bytes 1966080 | tf_op jit(solution)/shard_map/all_gather | solution.py:131
  172.6 100.3 %all-gather.10.cloned.1.call-start = ((), (), s32[]{:S(2)}) async-start(), calls=%async_computation.6 | async-start | bytes 8650752 | tf_op jit(solution)/shard_map/all_gather | solution.py:136
  173.1 169.4 %all-gather.12.cloned.1.call-start = ((), (), s32[]{:S(2)}) async-start(), calls=%async_computation.7 | async-start | bytes 8650752 | tf_op jit(solution)/shard_map/all_gather | solution.py:137
  173.7 238.5 %all-gather.14.cloned.1.call-start = ((), (), s32[]{:S(2)}) async-start(), calls=%async_computation.8 | async-start | bytes 8650752 | tf_op jit(solution)/shard_map/all_gather | solution.py:141
  174.3 293.2 %reduce-scatter.5.cloned.1.call-start = ((), (), s32[]{:S(2)}) async-start(), calls=%async_computation.9 | async-start | bytes 3932160 | tf_op jit(solution)/shard_map/reduce_scatter | solution.py:145
  412.2 57.2 %copy-start.1 = (bf16[512,2048]{1,0:T(8,128)(2,1)S(1)}, bf16[512,2048]{1,0:T(8,128)(2,1)}, u32[]{:S(2)}) copy-start(bf16[512,2048]{1,0:T(8,128)(2,1)} %param.20) | copy-start | bytes 6291460
Sparse Core Ops, SparseCore 0:
  16.3 27.0 all-gather.5
  108.2 61.6 reduce-scatter.2
  172.7 28.7 all-gather.7
  203.2 69.6 all-gather.9
  274.6 67.9 all-gather.11
  344.2 67.9 all-gather.13
  428.2 39.2 reduce-scatter.4
where the time goes:
time: 477 us; the launch traced here: 476 us
  waiting for transfers between devices  364 us (76%)
  matrix products  41 us (9%)
  local copies, waits for them, and re-layouts  27.2 us (6%)
  other arithmetic  16.8 us (4%)
  between operations  14.3 us (3%)
  starting transfers between devices  13 us (3%)
    all_gather x1, waiting for transfers between devices, local(): gate = add_rows(lax.all_gather(gate_weight, 'dp', axis=0, tiled=True))  71.4 us
    all_gather x1, waiting for transfers between devices, local(): lax.all_gather(down_weight, 'dp', axis=0, tiled=True)  69.7 us
    reduce_scatter x1, waiting for transfers between devices, local(): lax.psum_scatter(jnp.dot(mixed, output_weight, preferred_element_type=jnp...  61.6 us
    all_gather x1, waiting for transfers between devices, local(): upward = add_rows(lax.all_gather(up_weight, 'dp', axis=0, tiled=True))  60.6 us
    reduce_scatter x1, waiting for transfers between devices, local(): hidden_own = lax.psum_scatter(terms, 'mp', scatter_dimension=0, tiled=True)  39.4 us
    all_gather x1, waiting for transfers between devices, local(): normed_two = lax.all_gather(normed_own, 'mp', axis=0, tiled=True)  27.1 us
    ppermute x1, waiting for transfers between devices, swapped(): return lax.ppermute(value, axis, pairs)  25.3 us
    dot_general x1, matrix products, local(): lax.dot_general(activated, lax.all_gather(down_weight, 'dp', axis=0, tile...  15.9 us
  transfers between devices with their start and end apart: 9, of which 8 were waited for; matrix products, arithmetic and copies ran while one was open for 7% of the time, Pallas kernels for 0%

commit v1 on v0

--- a/solution.py
+++ b/solution.py
@@ -128,7 +128,12 @@
     )
     state_own = (tokens.astype(jnp.float32) + own_sum).astype(jnp.bfloat16)
     normed_own = layer_norm(state_own.astype(jnp.float32)).astype(jnp.bfloat16)
-    normed_two = lax.all_gather(normed_own, "mp", axis=0, tiled=True)
+    ring = [normed_own]
+    for hop in range(3):
+        ring.append(lax.ppermute(ring[-1], "mp", [(dev, (dev + 1) % 4) for dev in range(4)]))
+    normed_two = jnp.roll(
+        jnp.concatenate(ring[::-1], axis=0), (lax.axis_index("mp") + 1) * ring[0].shape[0], axis=0
+    )
 
     def add_rows(piece):
         return jnp.dot(normed_two, piece, preferred_element_type=jnp.float32)

time: 477 us -> 409 us (0.86)
  waiting for transfers between devices: 364 us -> 289 us
    all_gather x1, waiting for transfers between devices: 60.6 us -> 0.01 us  [local(): upward = add_rows(lax.all_gather(up_weight, 'dp', axis=0, tiled=True))]
    ppermute x0 -> x3, waiting for transfers between devices: none -> 30.9 us  [local(): lax.ppermute(ring[-1], 'mp', [(dev, (dev + 1) % 4) for dev in range(4)])]
    all_gather x1 -> x0, waiting for transfers between devices: 27.1 us -> none  [local(): normed_two = lax.all_gather(normed_own, 'mp', axis=0, tiled=True)]
    all_gather x1, waiting for transfers between devices: 69.7 us -> 53.3 us  [local(): lax.all_gather(down_weight, 'dp', axis=0, tiled=True)]
  transfers between devices with their start and end apart: 9 -> 11, of which waited for: 8 -> 9; matrix products, arithmetic and copies ran while one was open for 7% -> 10% of each run, Pallas kernels for 0% -> 0%
where the time goes in v1:
time: 409 us
  waiting for transfers between devices  289 us (71%)
  matrix products  41.1 us (10%)
  local copies, waits for them, and re-layouts  31.9 us (8%)
  other arithmetic  18 us (4%)
  between operations  15.6 us (4%)
  starting transfers between devices  13 us (3%)
    all_gather x1, waiting for transfers between devices, local(): gate = add_rows(lax.all_gather(gate_weight, 'dp', axis=0, tiled=True))  70.7 us
    reduce_scatter x1, waiting for transfers between devices, local(): lax.psum_scatter(jnp.dot(mixed, output_weight, preferred_element_type=jnp...  59.8 us
    all_gather x1, waiting for transfers between devices, local(): lax.all_gather(down_weight, 'dp', axis=0, tiled=True)  53.3 us
    reduce_scatter x1, waiting for transfers between devices, local(): hidden_own = lax.psum_scatter(terms, 'mp', scatter_dimension=0, tiled=True)  40 us
    ppermute x3, waiting for transfers between devices, local(): lax.ppermute(ring[-1], 'mp', [(dev, (dev + 1) % 4) for dev in range(4)])  30.9 us
    ppermute x1, waiting for transfers between devices, swapped(): return lax.ppermute(value, axis, pairs)  25.3 us
    dot_general x1, matrix products, local(): lax.dot_general(activated, lax.all_gather(down_weight, 'dp', axis=0, tile...  15.9 us
    reshape x1, local copies, waits for them, and re-layouts, local(): stored.reshape(stored.shape[0], 2, D)  9.46 us
  transfers between devices with their start and end apart: 11, of which 9 were waited for; matrix products, arithmetic and copies ran while one was open for 10% of the time, Pallas kernels for 0%

profile of v1, /device:TPU:1, one launch (start us, length us, event | category | flops | bytes accessed | tf_op | source)
XLA Modules:
  0.0 408.6 jit_solution(457913378124597812)
XLA Ops:
  7.4 1.8 copy.71
  9.1 7.8 %collective-permute-start = (bf16[128,4096]{0,1:T(8,128)(2,1)S(1)}, bf16[128,4096]{0,1:T(8,128)(2,1)}, u32[]{:S(2)}, u32[]{:S(2)}) collective-permute-start(bf16[128,4096]{0,1:T(8,128)(2,1)S(1)} %copy.71), channel_id=1, source_target_pairs={{0,128},{128,0},{1,129},{129,1},{2,130},{130,2},{3,131},{131,3},{4... | collective-permute-start | bytes 3145736 | tf_op jit(solution)/shard_map/ppermute | solution.py:19
  17.7 0.8 constant_dynamic-slice_fusion
  18.4 0.1 copy.86
  18.5 0.7 reduce
  19.2 0.1 convert_reduce_fusion.3
  19.3 0.2 reduce-window_1_clone.1
  19.5 0.2 reduce-window.9
  19.7 0.1 convert_reduce_fusion.2
  19.8 0.1 select_reduce_fusion
  19.9 0.2 broadcast_compare_fusion
  20.1 25.3 %collective-permute-done = bf16[128,4096]{0,1:T(8,128)(2,1)} collective-permute-done((bf16[128,4096]{0,1:T(8,128)(2,1)S(1)}, bf16[128,4096]{0,1:T(8,128)(2,1)}, u32[]{:S(2)}, u32[]{:S(2)}) %collective-permute-start) | collective-permute-done | bytes 1048608 | tf_op jit(solution)/shard_map/ppermute | solution.py:19
  45.4 1.3 broadcast_select_fusion
  46.7 9.5 %copy.73 = bf16[128,2,2048]{0,1,2:T(2,128)(2,1)} copy(bf16[128,2,2048]{0,2,1:T(8,128)(2,1)S(1)} %bitcast.26) | data formatting | bytes 2097152 | tf_op jit(solution)/shard_map/reshape | solution.py:101
  56.2 4.7 %all-to-all-start = ((bf16[128,2,2048]{0,1,2:T(2,128)(2,1)}), bf16[128,2,2048]{0,1,2:T(2,128)(2,1)S(1)}, u32[]{:S(2)}, u32[]{:S(2)}) async-start(bf16[128,2,2048]{0,1,2:T(2,128)(2,1)} %copy.73), calls=%async_computation | async-start | bytes 2097152 | tf_op jit(solution)/shard_map/all_to_all | solution.py:100
  60.9 0.1 fusion.35
  61.1 0.8 pad_add_fusion
  61.8 1.5 multiply_cosine_fusion
  63.3 7.3 %all-to-all-done = bf16[128,2,2048]{0,1,2:T(2,128)(2,1)S(1)} async-done(((bf16[128,2,2048]{0,1,2:T(2,128)(2,1)}), bf16[128,2,2048]{0,1,2:T(2,128)(2,1)S(1)}, u32[]{:S(2)}, u32[]{:S(2)}) %all-to-all-start) | async-done | bytes 1048608 | tf_op jit(solution)/shard_map/all_to_all | solution.py:100
  70.7 1.1 copy.74
  71.8 1.5 copy.75
  73.3 1.0 fusion.52
  74.3 1.3 copy.81
  75.5 0.3 copy.84
  75.8 2.0 copy.76
  77.9 1.8 convert_reduce_fusion
  79.7 2.0 fusion.4
  81.7 3.5 fusion.47
  85.2 1.4 reshape.153
  86.6 4.0 fusion.49
  90.6 2.3 reshape.151
  92.9 3.9 convolution_convert_fusion
  96.7 1.9 copy.85
  98.7 2.3 fusion.53
  101.0 0.4 subtract_convert_fusion.1
  101.4 0.9 fusion.26
  102.4 2.7 fusion.55
  105.2 1.1 fusion.16
  106.2 2.8 fusion.56
  109.1 0.5 all-gather.9.cloned.1.call-update
  109.7 0.5 all-gather.11.cloned.1.call-update
  110.2 0.5 all-gather.7.cloned.1.call-update
  110.8 0.3 reduce-scatter.5.cloned.1.call-start
  111.0 59.8 %reduce-scatter.3.cloned.1.call-done = f32[96,2048]{1,0:T(8,128)} async-done(((f32[384,2048]{1,0:T(8,128)}), f32[96,2048]{1,0:T(8,128)}) %reduce-scatter.3.cloned.1.call-update) | async-done | bytes 786448 | tf_op jit(solution)/shard_map/reduce_scatter | solution.py:123
  170.8 1.3 convert_reduce_fusion.1
  172.2 0.3 fusion.32
  172.5 0.2 fusion.33
  172.8 11.2 %collective-permute-done.1 = bf16[96,2048]{1,0:T(8,128)(2,1)S(1)} collective-permute-done((bf16[96,2048]{1,0:T(8,128)(2,1)S(1)}, bf16[96,2048]{1,0:T(8,128)(2,1)S(1)}, u32[]{:S(2)}, u32[]{:S(2)}) %collective-permute-start.1) | collective-permute-done | bytes 393248 | tf_op jit(solution)/shard_map/ppermute | solution.py:133
  184.0 10.3 %collective-permute-done.2 = bf16[96,2048]{1,0:T(8,128)(2,1)S(1)} collective-permute-done((bf16[96,2048]{1,0:T(8,128)(2,1)S(1)}, bf16[96,2048]{1,0:T(8,128)(2,1)S(1)}, u32[]{:S(2)}, u32[]{:S(2)}) %collective-permute-start.2) | collective-permute-done | bytes 393248 | tf_op jit(solution)/shard_map/ppermute | solution.py:133
  194.3 9.4 %collective-permute-done.3 = bf16[96,2048]{1,0:T(8,128)(2,1)S(1)} collective-permute-done((bf16[96,2048]{1,0:T(8,128)(2,1)S(1)}, bf16[96,2048]{1,0:T(8,128)(2,1)S(1)}, u32[]{:S(2)}, u32[]{:S(2)}) %collective-permute-start.3) | collective-permute-done | bytes 393248 | tf_op jit(solution)/shard_map/ppermute | solution.py:133
  203.7 0.8 constant_dynamic-update-slice_fusion.7
  204.5 0.8 constant_dynamic-update-slice_fusion.6
  205.3 0.8 constant_dynamic-update-slice_fusion.5
  206.1 1.0 constant_dynamic-update-slice_fusion.4
  207.1 0.8 constant_dynamic-update-slice_fusion.3
  207.9 0.8 constant_dynamic-update-slice_fusion.2
  208.6 0.8 constant_dynamic-update-slice_fusion.1
  209.4 1.0 constant_dynamic-update-slice_fusion
  210.4 9.0 %fusion.12 = f32[384,2048]{1,0:T(8,128)} fusion(bf16[2048,2048]{1,0:T(8,128)(2,1)} %all-gather.9.cloned.1.call-done, bf16[768,2048]{1,0:T(8,128)(2,1)} %constant_dynamic-update-slice_fusion, s32[]{:T(128)S(6)} %select_n.37), kind=kOutput, calls=%fused_computation.18 | convolution fusion | flops 3221225472 | bytes 13107204 | tf_op jit(solution)/shard_map/dot_general | solution.py:139
  219.5 53.3 %all-gather.11.cloned.1.call-done = bf16[2048,2048]{1,0:T(8,128)(2,1)} async-done(((bf16[64,2048]{1,0:T(8,128)(2,1)}), bf16[2048,2048]{1,0:T(8,128)(2,1)}) %all-gather.11.cloned.1.call-update) | async-done | bytes 8388624 | tf_op jit(solution)/shard_map/all_gather | solution.py:146
  272.8 70.7 %all-gather.7.cloned.1.call-done = bf16[2048,2048]{1,0:T(8,128)(2,1)} async-done(((bf16[64,2048]{1,0:T(8,128)(2,1)}), bf16[2048,2048]{1,0:T(8,128)(2,1)}) %all-gather.7.cloned.1.call-update) | async-done | bytes 8388624 | tf_op jit(solution)/shard_map/all_gather | solution.py:141
  343.4 15.9 %fusion.10 = f32[384,2048]{1,0:T(8,128)} fusion(bf16[2048,2048]{1,0:T(8,128)(2,1)} %all-gather.11.cloned.1.call-done, f32[384,2048]{1,0:T(8,128)} %fusion.12, bf16[2048,2048]{1,0:T(8,128)(2,1)} %all-gather.7.cloned.1.call-done, bf16[768,2048]{1,0:T(8,128)(2,1)} %constant_dynamic-update-slice_fusion, s32[]{:T(128)S(6)} %select_n.37), kind=kOutput, calls=%fused_computation.16 | convolution fusion | flops 6447169536 | bytes 24641540 | tf_op jit(solution)/shard_map/dot_general | solution.py:144
  359.3 40.0 %reduce-scatter.5.cloned.1.call-done = f32[96,2048]{1,0:T(8,128)} async-done(((f32[384,2048]{1,0:T(8,128)}), f32[96,2048]{1,0:T(8,128)}) %reduce-scatter.5.cloned.1.call-update) | async-done | bytes 786448 | tf_op jit(solution)/shard_map/reduce_scatter | solution.py:150
  399.3 2.0 fusion.34
  (38 shorter events, 0.4 us)
Async XLA Ops:
  7.4 98.9 %copy-start = (bf16[512,2048]{1,0:T(8,128)(2,1)S(1)}, bf16[512,2048]{1,0:T(8,128)(2,1)}, u32[]{:S(2)}) copy-start(bf16[512,2048]{1,0:T(8,128)(2,1)} %param.20) | copy-start | bytes 6291460
  7.4 70.5 %all-gather.5.cloned.1.call-start = ((), (), s32[]{:S(2)}) async-start(), calls=%async_computation.3 | async-start | bytes 1966080 | tf_op jit(solution)/shard_map/all_gather | solution.py:105
  9.1 36.3 %collective-permute-start = (bf16[128,4096]{0,1:T(8,128)(2,1)S(1)}, bf16[128,4096]{0,1:T(8,128)(2,1)}, u32[]{:S(2)}, u32[]{:S(2)}) collective-permute-start(bf16[128,4096]{0,1:T(8,128)(2,1)S(1)} %copy.71), channel_id=1, source_target_pairs={{0,128},{128,0},{1,129},{129,1},{2,130},{130,2},{3,131},{131,3},{4... | collective-permute-start | bytes 3145736 | tf_op jit(solution)/shard_map/ppermute | solution.py:19
  56.2 14.5 %all-to-all-start = ((bf16[128,2,2048]{0,1,2:T(2,128)(2,1)}), bf16[128,2,2048]{0,1,2:T(2,128)(2,1)S(1)}, u32[]{:S(2)}, u32[]{:S(2)}) async-start(bf16[128,2,2048]{0,1,2:T(2,128)(2,1)} %copy.73), calls=%async_computation | async-start | bytes 2097152 | tf_op jit(solution)/shard_map/all_to_all | solution.py:100
  60.9 109.9 %reduce-scatter.3.cloned.1.call-start = ((), (), s32[]{:S(2)}) async-start(), calls=%async_computation.4 | async-start | bytes 3932160 | tf_op jit(solution)/shard_map/reduce_scatter | solution.py:123
  77.9 3.8 copy-start.2
  98.7 2.3 copy-start.4
  98.7 2.3 copy-start.5
  101.4 1.0 copy-start.8
  102.4 2.7 copy-start.6
  102.4 2.7 copy-start.7
  109.0 61.8 %copy-start.3 = (bf16[96,2048]{1,0:T(8,128)(2,1)S(1)}, bf16[96,2048]{1,0:T(8,128)(2,1)}, u32[]{:S(2)}) copy-start(bf16[96,2048]{1,0:T(8,128)(2,1)} %param.12) | copy-start | bytes 1179652
  109.0 101.4 %all-gather.9.cloned.1.call-start = ((), (), s32[]{:S(2)}) async-start(), calls=%async_computation.6 | async-start | bytes 8650752 | tf_op jit(solution)/shard_map/all_gather | solution.py:142
  109.6 163.2 %all-gather.11.cloned.1.call-start = ((), (), s32[]{:S(2)}) async-start(), calls=%async_computation.7 | async-start | bytes 8650752 | tf_op jit(solution)/shard_map/all_gather | solution.py:146
  110.2 233.2 %all-gather.7.cloned.1.call-start = ((), (), s32[]{:S(2)}) async-start(), calls=%async_computation.5 | async-start | bytes 8650752 | tf_op jit(solution)/shard_map/all_gather | solution.py:141
  110.8 288.6 %reduce-scatter.5.cloned.1.call-start = ((), (), s32[]{:S(2)}) async-start(), calls=%async_computation.8 | async-start | bytes 3932160 | tf_op jit(solution)/shard_map/reduce_scatter | solution.py:150
  172.7 11.3 %collective-permute-start.1 = (bf16[96,2048]{1,0:T(8,128)(2,1)S(1)}, bf16[96,2048]{1,0:T(8,128)(2,1)S(1)}, u32[]{:S(2)}, u32[]{:S(2)}) collective-permute-start(bf16[96,2048]{1,0:T(8,128)(2,1)S(1)} %fusion.33), channel_id=1, source_target_pairs={{0,1},{1,2},{2,3},{3,0},{4,5},{5,6},{6,7},{7,4},{8,9},{9,10},{10,1... | collective-permute-start | bytes 1179656 | tf_op jit(solution)/shard_map/ppermute | solution.py:133
  184.0 10.3 %collective-permute-start.2 = (bf16[96,2048]{1,0:T(8,128)(2,1)S(1)}, bf16[96,2048]{1,0:T(8,128)(2,1)S(1)}, u32[]{:S(2)}, u32[]{:S(2)}) collective-permute-start(bf16[96,2048]{1,0:T(8,128)(2,1)S(1)} %collective-permute-done.1), channel_id=1, source_target_pairs={{0,1},{1,2},{2,3},{3,0},{4,5},{5,6},{6,7},{7,4},{8,9},{9,10},{10,1... | collective-permute-start | bytes 1179656 | tf_op jit(solution)/shard_map/ppermute | solution.py:133
  194.3 9.4 %collective-permute-start.3 = (bf16[96,2048]{1,0:T(8,128)(2,1)S(1)}, bf16[96,2048]{1,0:T(8,128)(2,1)S(1)}, u32[]{:S(2)}, u32[]{:S(2)}) collective-permute-start(bf16[96,2048]{1,0:T(8,128)(2,1)S(1)} %collective-permute-done.2), channel_id=1, source_target_pairs={{0,1},{1,2},{2,3},{3,0},{4,5},{5,6},{6,7},{7,4},{8,9},{9,10},{10,1... | collective-permute-start | bytes 1179656 | tf_op jit(solution)/shard_map/ppermute | solution.py:133
  343.4 57.9 %copy-start.1 = (bf16[512,2048]{1,0:T(8,128)(2,1)S(1)}, bf16[512,2048]{1,0:T(8,128)(2,1)}, u32[]{:S(2)}) copy-start(bf16[512,2048]{1,0:T(8,128)(2,1)} %param.20) | copy-start | bytes 6291460
Sparse Core Ops, SparseCore 0:
  17.1 27.0 all-gather.4
  109.1 61.6 reduce-scatter.2
  359.5 39.8 reduce-scatter.4
Sparse Core Ops, SparseCore 1:
  111.4 91.0 all-gather.8
  204.1 68.6 all-gather.10
  274.5 68.9 all-gather.6
